TPU v7x, 32 devices: a whole 2x2x4 slice. The times are simulated.
32 devices in a mesh: seq: 8 (over z, x), head: 4 (over y, core).
Axes of the slice: x: 2, y: 2, z: 4, core: 2. Of those that a mesh axis runs over, the one named last changes fastest.
Arguments:
- hidden: bfloat16 [1, 2048, 1024], P(None, 'seq'), may hold values from -6 to 6
- cotangent: bfloat16 [1, 2048, 1024], P(None, 'seq'), may hold values from -6 to 6
- pre_gain: float32 [1024], replicated, may hold values from 0.5 to 1.5
- w_zx: bfloat16 [1024, 2, 2048], P(None, None, 'head'), may hold values from -0.1875 to 0.1875
- w_bc: bfloat16 [1024, 256], replicated, may hold values from -0.1875 to 0.1875
- w_dt: bfloat16 [1024, 32], P(None, 'head'), may hold values from -0.1875 to 0.1875
- conv_x_w: float32 [4, 2048], P(None, 'head'), may hold values from -0.5 to 0.5
- conv_x_b: float32 [2048], P('head'), may hold values from -0.5 to 0.5
- conv_bc_w: float32 [4, 256], replicated, may hold values from -0.5 to 0.5
- conv_bc_b: float32 [256], replicated, may hold values from -0.5 to 0.5
- dt_bias: float32 [32], P('head'), may hold values from -4.5 to -2.5
- a_log: float32 [32], P('head'), as said below
- d_skip: float32 [32], P('head'), may hold values from 0.5 to 1.5
- gate_gain: float32 [2048], P('head'), may hold values from 0.5 to 1.5
- w_out: bfloat16 [2048, 1024], P('head'), may hold values from -0.125 to 0.125
Outputs:
- output: bfloat16 [1, 2048, 1024], P(None, 'seq')
- grad_hidden: float32 [1, 2048, 1024], P(None, 'seq')
- grad_pre_gain: float32 [1024], replicated
- grad_w_zx: float32 [1024, 2, 2048], P('seq', None, 'head')
- grad_w_bc: float32 [1024, 256], P('seq')
- grad_w_dt: float32 [1024, 32], P('seq', 'head')
- grad_conv_x_w: float32 [4, 2048], P(None, 'head')
- grad_conv_x_b: float32 [2048], P('head')
- grad_conv_bc_w: float32 [4, 256], replicated
- grad_conv_bc_b: float32 [256], replicated
- grad_dt_bias: float32 [32], P('head')
- grad_a_log: float32 [32], P('head')
- grad_d_skip: float32 [32], P('head')
- grad_gate_gain: float32 [2048], P('head')
- grad_w_out: float32 [2048, 1024], P('head', 'seq')
Inputs may be any that keep to these rules, and one draw needn't show every extreme that they name: Each head's decay rate exp(a_log) lies between 2.4 / 2048 and 2.
All inputs are finite; a program needn't handle non-finite values.
Results may differ from a plain program's by a relative error of at most 0.003.
The roundings to bfloat16 on the way count: a program that leaves them out, or rounds other values in their place, can miss the bound.
Values may be sent and summed in bfloat16 or wider, within the bound.
A program may use at most 128 MiB of HBM per device.

v0:
```python
import jax
import jax.numpy as jnp
from jax import lax
from jax.sharding import PartitionSpec as P

EPSILON = 1e-05
HIGHEST = lax.Precision.HIGHEST


def from_behind(value, axis, by):
    peers = lax.axis_size(axis)
    pairs = [(i, i + by) for i in range(peers) if 0 <= i + by < peers]
    return lax.ppermute(value, axis, pairs)


def entering(value, axis, join, neutral, backward):
    count, mine = (lax.axis_size(axis), lax.axis_index(axis))
    pieces = jax.tree.map(lambda part: lax.all_gather(part, axis), value)
    if backward:
        pieces = jax.tree.map(lambda part: part[::-1], pieces)
        mine = count - 1 - mine
    subtotal = jax.tree.map(
        lambda part, zero: jnp.full_like(part, 0) + jnp.asarray(zero, part.dtype), value, neutral
    )

    def hop(position, subtotal):
        longer = join(subtotal, jax.tree.map(lambda part: part[position], pieces))
        return jax.tree.map(lambda new, old: jnp.where(position < mine, new, old), longer, subtotal)

    return lax.fori_loop(0, count - 1, hop, subtotal)


def kept_low(values):
    return lax.optimization_barrier(values.astype(jnp.bfloat16)).astype(jnp.float32)


def silu_slope(values):
    sigmoid = jax.nn.sigmoid(values)
    return sigmoid * (1.0 + values * (1.0 - sigmoid))


def conv_apply(extended, weight, offset_b, length):
    summed = offset_b + weight[0] * extended[:, 0:length]
    for offset in range(1, weight.shape[0]):
        summed = summed + weight[offset] * extended[:, offset : offset + length]
    return summed


def conv_reverse(extended, weight, grad_pre, length):
    conv_reach = weight.shape[0] - 1
    grad_weight = jnp.stack(
        [
            jnp.sum(grad_pre * extended[:, offset : offset + length], axis=(0, 1))
            for offset in range(conv_reach + 1)
        ],
        0,
    )
    grad_offset = jnp.sum(grad_pre, axis=(0, 1))
    grad_ext = jnp.pad(weight[0] * grad_pre, ((0, 0), (0, conv_reach), (0, 0)))
    for offset in range(1, conv_reach + 1):
        grad_ext = grad_ext + jnp.pad(
            weight[offset] * grad_pre, ((0, 0), (offset, conv_reach - offset), (0, 0))
        )
    return (grad_weight, grad_offset, grad_ext)


def combine(earlier, later):
    return (earlier[0] * later[0], later[0][:, :, None, None] * earlier[1] + later[1])


def on_device(
    hidden,
    cotangent,
    pre_gain,
    w_zx,
    w_bc,
    w_dt,
    conv_x_w,
    conv_x_b,
    conv_bc_w,
    conv_bc_b,
    dt_bias,
    a_log,
    d_skip,
    gate_gain,
    w_out,
):
    seq_count, length, _ = hidden.shape
    head_count = dt_bias.shape[0]
    inner_dev = w_zx.shape[2]
    head_size = inner_dev // head_count
    states = w_bc.shape[1] // 2
    conv_reach = conv_x_w.shape[0] - 1
    full_inner = inner_dev * lax.axis_size("head")
    residual = hidden.astype(jnp.float32)
    in_rstd = lax.rsqrt(jnp.mean(residual * residual, axis=-1, keepdims=True) + EPSILON)
    normed_in = (residual * in_rstd * pre_gain).astype(jnp.bfloat16)
    projected = jnp.einsum("std,dke->stke", normed_in, w_zx, preferred_element_type=jnp.float32)
    gating = projected[:, :, 0]
    conv_in = projected[:, :, 1].astype(jnp.bfloat16)
    bc_in = jnp.einsum("std,dn->stn", normed_in, w_bc, preferred_element_type=jnp.float32).astype(
        jnp.bfloat16
    )
    dt_raw = jnp.einsum("std,dh->sth", normed_in, w_dt, preferred_element_type=jnp.float32)
    edge_x, edge_bc = from_behind(
        (conv_in[:, length - conv_reach :], bc_in[:, length - conv_reach :]), "seq", 1
    )
    ext_x = jnp.concatenate([edge_x, conv_in], 1).astype(jnp.float32)
    ext_bc = jnp.concatenate([edge_bc, bc_in], 1).astype(jnp.float32)
    pre_x = conv_apply(ext_x, conv_x_w, conv_x_b, length)
    pre_bc = conv_apply(ext_bc, conv_bc_w, conv_bc_b, length)
    x_heads = kept_low(jax.nn.silu(pre_x)).reshape(seq_count, length, head_count, head_size)
    bc_post = jax.nn.silu(pre_bc)
    b_mat = kept_low(bc_post[:, :, :states])
    c_mat = kept_low(bc_post[:, :, states:])
    deltas = jax.nn.softplus(dt_raw + dt_bias)
    rates = -jnp.exp(a_log)
    log_decay = deltas * rates
    cumulative = jnp.cumsum(log_decay, axis=1)
    last_cum = cumulative[:, -1]
    block_decay = jnp.exp(last_cum)
    tail_exp = jnp.exp(last_cum[:, None] - cumulative)
    tail_w = tail_exp * deltas
    weighted_x = tail_w[..., None] * x_heads
    local_state = jnp.einsum("sthp,stn->shpn", weighted_x, b_mat, precision=HIGHEST)
    empty_state = jnp.zeros_like(local_state)
    incoming = entering(
        (block_decay, local_state), "seq", combine, (jnp.ones_like(block_decay), empty_state), False
    )[1]
    scores = jnp.einsum("stn,sun->stu", c_mat, b_mat, precision=HIGHEST)
    row_ids = lax.broadcasted_iota(jnp.int32, (length, length), 0)
    column_ids = lax.broadcasted_iota(jnp.int32, (length, length), 1)
    causal = (row_ids >= column_ids)[None, :, :, None]
    spread = cumulative[:, :, None, :] - cumulative[:, None, :, :]
    decays = jnp.where(causal, jnp.exp(jnp.where(causal, spread, 0.0)), 0.0)
    weights = scores[..., None] * decays * deltas[:, None, :, :]
    inside = jnp.einsum("stuh,suhp->sthp", weights, x_heads, precision=HIGHEST)
    growth = jnp.exp(cumulative)
    from_state = jnp.einsum("stn,shpn->sthp", c_mat, incoming, precision=HIGHEST)
    outside = growth[..., None] * from_state
    ssd_out = inside + outside + d_skip[:, None] * x_heads
    flat_ssd = ssd_out.reshape(seq_count, length, inner_dev)
    gate_act = jax.nn.silu(gating)
    gated = flat_ssd * gate_act
    squares = lax.psum(jnp.sum(gated * gated, axis=-1), "head")
    gate_rstd = lax.rsqrt(squares / full_inner + EPSILON)[..., None]
    normed_out = (gated * gate_rstd * gate_gain).astype(jnp.bfloat16)
    partial_value = jnp.einsum("ste,ed->std", normed_out, w_out, preferred_element_type=jnp.float32)
    mixed = lax.psum(partial_value, "head")
    output = (residual + mixed).astype(jnp.bfloat16)
    grad_w_out = jnp.einsum(
        "ste,std->ed", normed_out, cotangent, preferred_element_type=jnp.float32
    )
    grad_normed = jnp.einsum("std,ed->ste", cotangent, w_out, preferred_element_type=jnp.float32)
    grad_gate_gain = jnp.sum(grad_normed * gated * gate_rstd, axis=(0, 1))
    scaled_out = grad_normed * gate_gain
    dotted = lax.psum(jnp.sum(scaled_out * gated, axis=-1), "head")
    grad_gated = gate_rstd * scaled_out - gated * gate_rstd**3 * (dotted / full_inner)[..., None]
    grad_ssd = (grad_gated * gate_act).reshape(seq_count, length, head_count, head_size)
    grad_gating = grad_gated * flat_ssd * silu_slope(gating)
    grad_d_skip = jnp.sum(grad_ssd * x_heads, axis=(0, 1, 3))
    grad_x = d_skip[:, None] * grad_ssd
    grad_from = growth[..., None] * grad_ssd
    grad_cum = jnp.sum(grad_ssd * outside, axis=-1)
    state_grad_local = jnp.einsum("sthp,stn->shpn", grad_from, c_mat, precision=HIGHEST)
    grad_c = jnp.einsum("sthp,shpn->stn", grad_from, incoming, precision=HIGHEST)
    after = entering(
        (block_decay, state_grad_local),
        "seq",
        combine,
        (jnp.ones_like(block_decay), empty_state),
        True,
    )[1]
    grad_last = jnp.sum(after * incoming, axis=(2, 3)) * block_decay
    grad_weighted = jnp.einsum("shpn,stn->sthp", after, b_mat, precision=HIGHEST)
    grad_b = jnp.einsum("sthp,shpn->stn", weighted_x, after, precision=HIGHEST)
    grad_x = grad_x + tail_w[..., None] * grad_weighted
    grad_tail = jnp.sum(grad_weighted * x_heads, axis=-1)
    grad_last = grad_last + jnp.sum(grad_tail * tail_w, axis=1)
    grad_cum = grad_cum - grad_tail * tail_w
    grad_deltas = grad_tail * tail_exp
    grad_weights = jnp.einsum("sthp,suhp->stuh", grad_ssd, x_heads, precision=HIGHEST)
    grad_x = grad_x + jnp.einsum("stuh,sthp->suhp", weights, grad_ssd, precision=HIGHEST)
    grad_scores = jnp.sum(grad_weights * decays * deltas[:, None, :, :], axis=-1)
    exponent_grad = grad_weights * weights
    grad_cum = grad_cum + jnp.sum(exponent_grad, axis=2) - jnp.sum(exponent_grad, axis=1)
    grad_deltas = grad_deltas + jnp.sum(grad_weights * scores[..., None] * decays, axis=1)
    grad_c = grad_c + jnp.einsum("stu,sun->stn", grad_scores, b_mat, precision=HIGHEST)
    grad_b = grad_b + jnp.einsum("stu,stn->sun", grad_scores, c_mat, precision=HIGHEST)
    grad_cum = grad_cum.at[:, -1].add(grad_last)
    grad_log_decay = jnp.flip(jnp.cumsum(jnp.flip(grad_cum, 1), axis=1), 1)
    grad_a_log = rates * jnp.sum(grad_log_decay * deltas, axis=(0, 1))
    grad_u = (grad_deltas + grad_log_decay * rates) * jax.nn.sigmoid(dt_raw + dt_bias)
    grad_dt_bias = jnp.sum(grad_u, axis=(0, 1))
    grad_dt_raw = grad_u.astype(jnp.bfloat16)
    grad_bc_post = lax.psum(jnp.concatenate([grad_b, grad_c], -1), "head")
    grad_pre_x = grad_x.reshape(seq_count, length, inner_dev) * silu_slope(pre_x)
    grad_pre_bc = grad_bc_post * silu_slope(pre_bc)
    grad_conv_x_w, grad_conv_x_b, grad_ext_x = conv_reverse(ext_x, conv_x_w, grad_pre_x, length)
    grad_conv_bc_w, grad_conv_bc_b, grad_ext_bc = conv_reverse(
        ext_bc, conv_bc_w, grad_pre_bc, length
    )
    sent_x, sent_bc = from_behind(
        (grad_ext_x[:, :conv_reach], grad_ext_bc[:, :conv_reach]), "seq", -1
    )
    tail_pad = ((0, 0), (length - conv_reach, 0), (0, 0))
    grad_conv_in = grad_ext_x[:, conv_reach:] + jnp.pad(sent_x, tail_pad)
    grad_bc_in = (grad_ext_bc[:, conv_reach:] + jnp.pad(sent_bc, tail_pad)).astype(jnp.bfloat16)
    grad_projected = jnp.stack([grad_gating, grad_conv_in], 2).astype(jnp.bfloat16)
    grad_w_zx = jnp.einsum(
        "std,stke->dke", normed_in, grad_projected, preferred_element_type=jnp.float32
    )
    grad_w_bc = jnp.einsum("std,stn->dn", normed_in, grad_bc_in, preferred_element_type=jnp.float32)
    grad_w_dt = jnp.einsum(
        "std,sth->dh", normed_in, grad_dt_raw, preferred_element_type=jnp.float32
    )
    head_part = jnp.einsum(
        "stke,dke->std", grad_projected, w_zx, preferred_element_type=jnp.float32
    )
    head_part = head_part + jnp.einsum(
        "sth,dh->std", grad_dt_raw, w_dt, preferred_element_type=jnp.float32
    )
    grad_normed_in = lax.psum(head_part, "head")
    grad_normed_in = grad_normed_in + jnp.einsum(
        "stn,dn->std", grad_bc_in, w_bc, preferred_element_type=jnp.float32
    )
    grad_pre_gain = jnp.sum(grad_normed_in * residual * in_rstd, axis=(0, 1))
    scaled_in = grad_normed_in * pre_gain
    grad_hidden = (
        cotangent.astype(jnp.float32)
        + in_rstd * scaled_in
        - residual * in_rstd**3 * jnp.mean(scaled_in * residual, axis=-1, keepdims=True)
    )
    weight_sums = (
        lax.psum_scatter(grad_w_zx, "seq", scatter_dimension=0, tiled=True),
        lax.psum_scatter(grad_w_bc, "seq", scatter_dimension=0, tiled=True),
        lax.psum_scatter(grad_w_dt, "seq", scatter_dimension=0, tiled=True),
        lax.psum_scatter(grad_w_out, "seq", scatter_dimension=1, tiled=True),
    )
    minor_sums = lax.psum(
        (
            grad_pre_gain,
            grad_conv_x_w,
            grad_conv_x_b,
            grad_conv_bc_w,
            grad_conv_bc_b,
            grad_dt_bias,
            grad_a_log,
            grad_d_skip,
            grad_gate_gain,
        ),
        "seq",
    )
    return (
        output,
        grad_hidden,
        minor_sums[0],
        weight_sums[0],
        weight_sums[1],
        weight_sums[2],
        minor_sums[1],
        minor_sums[2],
        minor_sums[3],
        minor_sums[4],
        minor_sums[5],
        minor_sums[6],
        minor_sums[7],
        minor_sums[8],
        weight_sums[3],
    )


def solution(mesh):
    return jax.shard_map(
        on_device,
        mesh=mesh,
        in_specs=(
            P(None, "seq", None),
            P(None, "seq", None),
            P(),
            P(None, None, "head"),
            P(),
            P(None, "head"),
            P(None, "head"),
            P("head"),
            P(),
            P(),
            P("head"),
            P("head"),
            P("head"),
            P("head"),
            P("head", None),
        ),
        out_specs=(
            P(None, "seq", None),
            P(None, "seq", None),
            P(),
            P("seq", None, "head"),
            P("seq", None),
            P("seq", "head"),
            P(None, "head"),
            P("head"),
            P(),
            P(),
            P("head"),
            P("head"),
            P("head"),
            P("head"),
            P("head", "seq"),
        ),
        check_vma=False,
    )
```

profile of v0, /device:TPU:0, one launch (start us, length us, event | category | flops | bytes accessed | tf_op | source)
XLA Modules:
  0.0 565.5 jit_solution(15895205505120907254)
XLA Ops:
  7.3 1.4 fusion.30
  9.2 1.6 fusion.27
  10.8 5.0 collective-permute-start.1
  16.7 3.5 collective-permute-start
  25.7 1.1 multiply_convert_fusion.2
  27.7 2.1 copy.117
  29.8 2.1 fusion.88
  32.0 1.9 slice.180
  33.8 1.3 copy.115
  35.9 2.1 copy.124
  38.0 2.0 copy.121
  40.0 18.9 %all_gather.18 = f32[8,1,8]{2,1,0:T(1,128)} all-gather(f32[1,1,8]{2,1,0:T(1,128)} %copy.115), channel_id=1, replica_groups=mesh['seq'=8,'head'=4] {'seq'}, dimensions={0}, use_global_device_ids=true | all-gather | bytes 288 | tf_op jit(solution)/shard_map/all_gather | solution.py:18
  59.6 1.3 fusion.103
  60.9 1.7 fusion.94
  64.4 17.0 %all-gather.5.cloned.1.call-done = f32[64,64,128]{2,1,0:T(8,128)} async-done(((f32[8,64,128]{2,1,0:T(8,128)}), f32[64,64,128]{2,1,0:T(8,128)}) %all-gather.5.cloned.1.call-update) | async-done | bytes 2097168 | tf_op jit(solution)/shard_map/all_gather | solution.py:18
  81.4 11.9 %while.29 = (s32[]{:T(128)}, f32[1,8,64,128]{3,2,1,0:T(8,128)S(1)}, s32[]{:T(128)}, f32[8,1,8]{2,1,0:T(1,128)}, f32[8,1,8,64,128]{4,3,2,1,0:T(8,128)}, /*index=5*/s32[]{:T(128)}, s32[]{:T(128)}) while((s32[]{:T(128)}, f32[1,8,64,128]{3,2,1,0:T(8,128)S(1)}, s32[]{:T(128)}, f32[8,1,8]{2,1,0:T(1,128)}, ...), condition=%wide.region_4.5_spmd.clone, body=%wide.region_3.4_spmd.clone.sunk | while | flops 262148 | bytes 786641 | solution.py:30
  93.8 4.4 multiply_reduce_fusion.8
  98.2 5.6 psum.98
  103.9 2.1 copy.120
  106.0 3.8 multiply_reduce_fusion
  109.8 7.1 %psum.100 = f32[1,256]{1,0:T(1,128)} all-reduce(f32[1,256]{1,0:T(1,128)S(1)} %bitcast.383), channel_id=1, replica_groups=mesh['seq'=8,'head'=4] {'head'}, use_global_device_ids=true, to_apply=%region_9.10 | all-reduce | flops 256 | bytes 2048 | tf_op jit(solution)/shard_map/psum | solution.py:157
  117.6 2.2 fusion.52
  121.6 2.1 copy.125
  123.6 2.1 fusion.90
  126.6 2.0 copy.123
  128.6 2.0 convolution_bitcast_fusion.2
  130.7 4.2 fusion.23
  136.3 1.5 convolution_bitcast_fusion.1
  138.9 34.3 %all-gather.7.cloned.1.call-done = f32[64,64,128]{2,1,0:T(8,128)} async-done(((f32[8,64,128]{2,1,0:T(8,128)}), f32[64,64,128]{2,1,0:T(8,128)}) %all-gather.7.cloned.1.call-update) | async-done | bytes 2097168 | tf_op jit(solution)/shard_map/all_gather | solution.py:18
  173.2 3.1 rev.14
  176.3 12.1 %while.30 = (s32[]{:T(128)}, f32[1,8,64,128]{3,2,1,0:T(8,128)S(1)}, s32[]{:T(128)}, f32[8,1,8]{2,1,0:T(1,128)}, f32[8,1,8,64,128]{4,3,2,1,0:T(8,128)}, /*index=5*/s32[]{:T(128)}, s32[]{:T(128)}) while((s32[]{:T(128)}, f32[1,8,64,128]{3,2,1,0:T(8,128)S(1)}, s32[]{:T(128)}, f32[8,1,8]{2,1,0:T(1,128)}, ...), condition=%wide.region_11.12_spmd.clone, body=%wide.region_10.11_spmd.clone.sunk | while | flops 262148 | bytes 786641 | solution.py:30
  177.0 1.0 fusion.150
  178.7 1.0 fusion.150
  180.4 1.0 fusion.150
  182.2 1.0 fusion.150
  183.9 1.0 fusion.150
  185.6 1.0 fusion.150
  188.5 2.8 convolution_bitcast_fusion.3
  191.9 1.5 multiply_reduce_fusion.6
  193.5 2.8 fusion.24
  196.3 2.0 copy.127
  198.3 2.2 multiply_reduce_fusion.4
  200.9 1.0 pad_add_fusion
  204.6 1.3 collective-permute-start.2
  206.9 1.6 pad_maximum_fusion.3
  208.5 1.7 collective-permute-done.2
  210.2 1.1 fusion.74
  212.1 1.3 fusion.18
  213.5 2.8 fusion.64
  216.6 1.2 multiply_convert_fusion
  218.8 2.9 fusion.53
  221.7 47.0 %all-reduce.14.cloned.1.call-done = (f32[1,256,1024]{2,1,0:T(8,128)}, f32[1,256,1024]{2,1,0:T(8,128)}, f32[1,256,256]{2,1,0:T(8,128)}) async-done(((f32[1,256,1024]{2,1,0:T(8,128)}, f32[1,256,1024]{2,1,0:T(8,128)}, f32[1,256,256]{2,1,0:T(8,128)}), (f32[1,256,1024]{2,1,0:T(8,128)}, f32[1,256,1024]{2,1,0:T(8,128)}, f32[1,256,256]{2,1,0:T(8,128)})) %all-reduce.14.cloned.1.call-update) | async-done | bytes 2359312 | tf_op jit(solution)/shard_map/psum | solution.py:149
  268.7 1.2 multiply_reduce_fusion.12
  270.1 1.4 collective-permute-start.3
  271.6 4.1 collective-permute-done.3
  275.7 1.5 fusion.67
  277.5 2.9 fusion.38
  280.4 37.8 %all-reduce.10 = (f32[1024]{0:T(1024)}, f32[4,512]{1,0:T(4,128)}, f32[512]{0:T(512)}, f32[4,256]{1,0:T(4,128)}, f32[256]{0:T(256)}, /*index=5*/f32[8]{0:T(128)}, f32[8]{0:T(128)}, f32[8]{0:T(128)}, f32[512]{0:T(512)}) all-reduce(f32[1024]{0:T(1024)S(1)} %get-tuple-element.347, ...), channel_id=1, replica_groups=mesh['seq'=8,'head'=4] {'seq'}, use_global_device_ids=true, to_apply=%region_26.27 | all-reduce | flops 5400 | bytes 43200 | tf_op jit(solution)/shard_map/psum | solution.py:240
  318.2 3.3 fusion.35
  321.5 39.8 %reduce-scatter.5.cloned.1.call-done = f32[128,2,512]{2,0,1:T(8,128)} async-done(((f32[1024,2,512]{2,0,1:T(8,128)}), f32[128,2,512]{2,0,1:T(8,128)}) %reduce-scatter.5.cloned.1.call-update) | async-done | bytes 524304 | tf_op jit(solution)/shard_map/reduce_scatter | solution.py:235
  361.3 2.2 copy.137
  363.5 55.7 %reduce-scatter.9.cloned.1.call-done = f32[128,8]{0,1:T(8,128)} async-done(((f32[1024,8]{0,1:T(8,128)}), f32[128,8]{0,1:T(8,128)}) %reduce-scatter.9.cloned.1.call-update) | async-done | bytes 4112 | tf_op jit(solution)/shard_map/reduce_scatter | solution.py:237
  419.3 72.1 %reduce-scatter.11.cloned.1.call-done = f32[512,128]{1,0:T(8,128)} async-done(((f32[512,1024]{1,0:T(8,128)}), f32[512,128]{1,0:T(8,128)}) %reduce-scatter.11.cloned.1.call-update) | async-done | bytes 262160 | tf_op jit(solution)/shard_map/reduce_scatter | solution.py:238
  491.3 67.3 %reduce-scatter.7.cloned.1.call-done = f32[128,256]{1,0:T(8,128)} async-done(((f32[1024,256]{1,0:T(8,128)}), f32[128,256]{1,0:T(8,128)}) %reduce-scatter.7.cloned.1.call-update) | async-done | bytes 131088 | tf_op jit(solution)/shard_map/reduce_scatter | solution.py:236
  (244 shorter events, 41.6 us)
Async XLA Ops:
  7.2 8.7 %copy-start = (bf16[1024,2,512]{2,1,0:T(2,128)(2,1)S(1)}, bf16[1024,2,512]{2,1,0:T(2,128)(2,1)}, u32[]{:S(2)}) copy-start(bf16[1024,2,512]{2,1,0:T(2,128)(2,1)} %param.24) | copy-start | bytes 6291460
  7.2 8.7 %copy-start.1 = (bf16[1,256,1024]{2,1,0:T(8,128)(2,1)S(1)}, bf16[1,256,1024]{2,1,0:T(8,128)(2,1)}, u32[]{:S(2)}) copy-start(bf16[1,256,1024]{2,1,0:T(8,128)(2,1)} %param.21) | copy-start | bytes 1572868
  7.2 8.7 %copy-start.25 = (f32[1024]{0:T(1024)S(1)}, f32[1024]{0:T(1024)}, u32[]{:S(2)}) copy-start(f32[1024]{0:T(1024)} %param.23) | copy-start | bytes 12292
  7.2 74.2 %all-gather.5.cloned.1.call-start = ((), (), s32[]{:S(2)}) async-start(), calls=%async_computation.8 | async-start | bytes 2359296 | tf_op jit(solution)/shard_map/all_gather | solution.py:18
  10.8 9.4 %copy-start.67 = (f32[8]{0:T(128)S(1)}, f32[8]{0:T(128)}, u32[]{:S(2)}) copy-start(f32[8]{0:T(128)} %param.32) | copy-start | bytes 100
  10.8 9.4 %copy-start.54 = (f32[4,512]{1,0:T(4,128)S(1)}, f32[4,512]{1,0:T(4,128)}, u32[]{:S(2)}) copy-start(f32[4,512]{1,0:T(4,128)} %param.27) | copy-start | bytes 24580
  10.8 9.4 %copy-start.31 = (bf16[1024,8]{0,1:T(8,128)(2,1)S(1)}, bf16[1024,8]{0,1:T(8,128)(2,1)}, u32[]{:S(2)}) copy-start(bf16[1024,8]{0,1:T(8,128)(2,1)} %param.26) | copy-start | bytes 49156
  10.8 9.4 %copy-start.64 = (f32[8]{0:T(128)S(1)}, f32[8]{0:T(128)}, u32[]{:S(2)}) copy-start(f32[8]{0:T(128)} %param.31) | copy-start | bytes 100
  10.8 12.6 %copy-start.57 = (f32[4,256]{1,0:T(4,128)S(1)}, f32[4,256]{1,0:T(4,128)}, u32[]{:S(2)}) copy-start(f32[4,256]{1,0:T(4,128)} %param.29) | copy-start | bytes 12292
  10.8 13.8 %collective-permute-start.1 = (bf16[1,3,256]{2,1,0:T(4,128)(2,1)S(1)}, bf16[1,3,256]{2,1,0:T(4,128)(2,1)S(1)}, u32[]{:S(2)}, u32[]{:S(2)}) collective-permute-start(bf16[1,3,256]{2,1,0:T(4,128)(2,1)S(1)} %slice.171), channel_id=1, source_target_pairs={{0,4},{4,8},{8,12},{12,16},{16,20},{20,24},{24,28},{1,5},{5,9},{9,... | collective-permute-start | bytes 4616 | tf_op jit(solution)/shard_map/ppermute | solution.py:13
  16.6 4.0 copy-start.5
  16.7 8.0 %copy-start.63 = (f32[256]{0:T(256)S(1)}, f32[256]{0:T(256)}, u32[]{:S(2)}) copy-start(f32[256]{0:T(256)} %param.30) | copy-start | bytes 3076
  16.7 8.8 %collective-permute-start = (bf16[1,3,512]{2,1,0:T(4,128)(2,1)S(1)}, bf16[1,3,512]{2,1,0:T(4,128)(2,1)S(1)}, u32[]{:S(2)}, u32[]{:S(2)}) collective-permute-start(bf16[1,3,512]{2,1,0:T(4,128)(2,1)S(1)} %slice.166), channel_id=1, source_target_pairs={{0,4},{4,8},{8,12},{12,16},{16,20},{20,24},{24,28},{1,5},{5,9},{9,... | collective-permute-start | bytes 9224 | tf_op jit(solution)/shard_map/ppermute | solution.py:13
  20.3 5.4 copy-start.27
  20.3 5.4 copy-start.29
  25.5 4.2 copy-start.15
  31.9 141.3 %all-gather.7.cloned.1.call-start = ((), (), s32[]{:S(2)}) async-start(), calls=%async_computation.9 | async-start | bytes 2359296 | tf_op jit(solution)/shard_map/all_gather | solution.py:18
  81.4 12.3 %copy-start.65 = (f32[8]{0:T(128)S(1)}, f32[8]{0:T(128)}, u32[]{:S(2)}) copy-start(f32[8]{0:T(128)} %param.33) | copy-start | bytes 100
  93.8 4.5 copy-start.10
  93.8 12.2 %copy-start.26 = (f32[512]{0:T(512)S(1)}, f32[512]{0:T(512)}, u32[]{:S(2)}) copy-start(f32[512]{0:T(512)} %param.34) | copy-start | bytes 6148
  103.9 13.7 %copy-start.34 = (f32[256]{0:T(256)}, f32[256]{0:T(256)S(1)}, u32[]{:S(2)}) copy-start(f32[256]{0:T(256)S(1)} %multiply_multiply_fusion.17) | copy-start | bytes 3076
  116.9 3.8 copy-start.7
  117.6 6.0 %copy-start.36 = (f32[1,256]{1,0:T(1,128)}, f32[1,256]{1,0:T(1,128)S(1)}, u32[]{:S(2)}) copy-start(f32[1,256]{1,0:T(1,128)S(1)} %broadcast_multiply_fusion.8) | copy-start | bytes 3076
  119.9 6.1 %copy-start.33 = (f32[8,1,8]{2,1,0:T(1,128)S(1)}, f32[8,1,8]{2,1,0:T(1,128)}, u32[]{:S(2)}) copy-start(f32[8,1,8]{2,1,0:T(1,128)} %get-tuple-element.585) | copy-start | bytes 772
  125.8 142.9 %all-reduce.14.cloned.1.call-start = ((), (), s32[]{:S(2)}) async-start(), calls=%async_computation.10 | async-start | bytes 4718592 | tf_op jit(solution)/shard_map/psum | solution.py:149
  130.7 4.3 copy-start.16
  130.7 5.3 copy-start.8
  130.7 5.3 copy-start.11
  130.7 5.3 copy-start.4
  135.0 2.9 copy-start.20
  135.0 2.9 copy-start.6
  135.0 2.9 copy-start.12
  135.0 2.9 copy-start.14
  135.0 2.9 copy-start.35
  135.0 2.9 copy-start.37
  188.4 5.0 copy-start.9
  188.4 5.0 copy-start.23
  188.4 5.0 copy-start.24
  188.5 5.0 copy-start.53
  188.5 5.0 copy-start.55
  188.5 5.0 copy-start.66
  198.3 2.2 copy-start.28
  198.3 2.2 copy-start.30
  200.9 10.4 %copy-start.18 = (bf16[256,1,512]{2,0,1:T(8,128)(2,1)S(1)}, bf16[256,1,512]{2,0,1:T(8,128)(2,1)}, u32[]{:S(2)}) copy-start(bf16[256,1,512]{2,0,1:T(8,128)(2,1)} %fusion.84) | copy-start | bytes 786436
  204.6 5.5 collective-permute-start.2
  213.4 147.9 %reduce-scatter.5.cloned.1.call-start = ((), (), s32[]{:S(2)}) async-start(), calls=%async_computation.4 | async-start | bytes 4718592 | tf_op jit(solution)/shard_map/reduce_scatter | solution.py:235
  216.3 203.0 %reduce-scatter.9.cloned.1.call-start = ((), (), s32[]{:S(2)}) async-start(), calls=%async_computation.6 | async-start | bytes 36864 | tf_op jit(solution)/shard_map/reduce_scatter | solution.py:237
  218.7 272.6 %reduce-scatter.11.cloned.1.call-start = ((), (), s32[]{:S(2)}) async-start(), calls=%async_computation.7 | async-start | bytes 2359296 | tf_op jit(solution)/shard_map/reduce_scatter | solution.py:238
  218.8 49.9 %copy-start.17 = (f32[1,256,256]{2,1,0:T(8,128)S(1)}, f32[1,256,256]{2,1,0:T(8,128)}, u32[]{:S(2)}) copy-start(f32[1,256,256]{2,1,0:T(8,128)} %get-tuple-element.405) | copy-start | bytes 786436
  221.7 48.2 %copy-start.39 = (f32[1,256]{1,0:T(1,128)S(1)}, f32[1,256]{1,0:T(1,128)}, u32[]{:S(2)}) copy-start(f32[1,256]{1,0:T(1,128)} %copy-done.38) | copy-start | bytes 3076
  221.7 48.2 %copy-start.41 = (f32[1,256]{1,0:T(1,128)S(1)}, f32[1,256]{1,0:T(1,128)}, u32[]{:S(2)}) copy-start(f32[1,256]{1,0:T(1,128)} %copy-done.40) | copy-start | bytes 3076
  221.7 48.2 %copy-start.43 = (f32[1,256]{1,0:T(1,128)S(1)}, f32[1,256]{1,0:T(1,128)}, u32[]{:S(2)}) copy-start(f32[1,256]{1,0:T(1,128)} %copy-done.42) | copy-start | bytes 3076
  221.7 48.2 %copy-start.45 = (f32[1,256]{1,0:T(1,128)S(1)}, f32[1,256]{1,0:T(1,128)}, u32[]{:S(2)}) copy-start(f32[1,256]{1,0:T(1,128)} %copy-done.44) | copy-start | bytes 3076
  221.7 337.0 %reduce-scatter.7.cloned.1.call-start = ((), (), s32[]{:S(2)}) async-start(), calls=%async_computation.5 | async-start | bytes 1179648 | tf_op jit(solution)/shard_map/reduce_scatter | solution.py:236
  270.0 7.2 %copy-start.47 = (f32[512]{0:T(512)S(1)}, f32[512]{0:T(512)}, u32[]{:S(2)}) copy-start(f32[512]{0:T(512)} %get-tuple-element.393) | copy-start | bytes 6148
  270.0 7.4 %copy-start.49 = (f32[512]{0:T(512)S(1)}, f32[512]{0:T(512)}, u32[]{:S(2)}) copy-start(f32[512]{0:T(512)} %get-tuple-element.349) | copy-start | bytes 6148
  270.0 7.4 %copy-start.50 = (f32[512]{0:T(512)S(1)}, f32[512]{0:T(512)}, u32[]{:S(2)}) copy-start(f32[512]{0:T(512)} %get-tuple-element.350) | copy-start | bytes 6148
  270.1 7.4 %copy-start.51 = (f32[512]{0:T(512)S(1)}, f32[512]{0:T(512)}, u32[]{:S(2)}) copy-start(f32[512]{0:T(512)} %get-tuple-element.351) | copy-start | bytes 6148
  270.1 7.4 %copy-start.52 = (f32[512]{0:T(512)S(1)}, f32[512]{0:T(512)}, u32[]{:S(2)}) copy-start(f32[512]{0:T(512)} %get-tuple-element.352) | copy-start | bytes 6148
  270.1 7.4 %copy-start.68 = (f32[8]{0:T(128)S(1)}, f32[8]{0:T(128)}, u32[]{:S(2)}) copy-start(f32[8]{0:T(128)} %param.32) | copy-start | bytes 100
  270.1 5.6 collective-permute-start.3
  277.2 3.2 copy-start.48
  277.2 3.2 copy-start.62
  277.2 41.0 %copy-start.58 = (f32[256]{0:T(256)S(1)}, f32[256]{0:T(256)}, u32[]{:S(2)}) copy-start(f32[256]{0:T(256)} %get-tuple-element.435) | copy-start | bytes 3076
  (16 other events, 23.2 us)
Sparse Core Ops, SparseCore 0:
  32.0 49.3 all-gather.4
  125.9 47.2 all-gather.6
  213.5 55.1 all-reduce.13
  272.2 89.0 reduce-scatter.4
  364.8 54.3 reduce-scatter.8
  423.2 68.0 reduce-scatter.10
  495.3 63.2 reduce-scatter.6
where the time goes:
time: 568 us; the launch traced here: 566 us
  waiting for transfers between devices  339 us (60%)
  blocking collectives  69.5 us (12%)
  matrix products  46.3 us (8%)
  other arithmetic  43.3 us (8%)
  local copies, waits for them, and re-layouts  40 us (7%)
  between operations  15.2 us (3%)
  starting transfers between devices  11.8 us (2%)
    reduce_scatter x1, waiting for transfers between devices, on_device(): lax.psum_scatter(grad_w_out, 'seq', scatter_dimension=1, tiled=True)  72.1 us
    reduce_scatter x1, waiting for transfers between devices, on_device(): lax.psum_scatter(grad_w_bc, 'seq', scatter_dimension=0, tiled=True)  67.3 us
    reduce_scatter x1, waiting for transfers between devices, on_device(): lax.psum_scatter(grad_w_dt, 'seq', scatter_dimension=0, tiled=True)  55.7 us
    all_gather x2, waiting for transfers between devices, entering(): pieces = jax.tree.map(lambda part: lax.all_gather(part, axis), value)  51.3 us
    psum x1, waiting for transfers between devices, on_device(): mixed = lax.psum(partial_value, 'head')  47 us
    reduce_scatter x1, waiting for transfers between devices, on_device(): lax.psum_scatter(grad_w_zx, 'seq', scatter_dimension=0, tiled=True)  39.8 us
    psum x1, blocking collectives, on_device(): lax.psum((grad_pre_gain, grad_conv_x_w, grad_conv_x_b, grad_conv_bc_w, gr...  37.8 us
    all_gather x1, blocking collectives, entering(): pieces = jax.tree.map(lambda part: lax.all_gather(part, axis), value)  18.9 us
  transfers between devices with their start and end apart: 11, of which 9 were waited for; matrix products, arithmetic and copies ran while one was open for 9% of the time, Pallas kernels for 0%

commit v1 on v0

--- a/solution.py
+++ b/solution.py
@@ -1,7 +1,16 @@
+import functools
+
 import jax
 import jax.numpy as jnp
 from jax import lax
+from jax.experimental import pallas as pl
+from jax.experimental.pallas import tpu as pltpu
 from jax.sharding import PartitionSpec as P
+
+MESH = pl.DeviceIdType.MESH
+VMEM = pltpu.VMEM
+DMA = pltpu.SemaphoreType.DMA
+IN_VMEM = pl.BlockSpec(memory_space=pltpu.VMEM)
 
 EPSILON = 1e-05
 HIGHEST = lax.Precision.HIGHEST
@@ -11,23 +20,6 @@
     peers = lax.axis_size(axis)
     pairs = [(i, i + by) for i in range(peers) if 0 <= i + by < peers]
     return lax.ppermute(value, axis, pairs)
-
-
-def entering(value, axis, join, neutral, backward):
-    count, mine = (lax.axis_size(axis), lax.axis_index(axis))
-    pieces = jax.tree.map(lambda part: lax.all_gather(part, axis), value)
-    if backward:
-        pieces = jax.tree.map(lambda part: part[::-1], pieces)
-        mine = count - 1 - mine
-    subtotal = jax.tree.map(
-        lambda part, zero: jnp.full_like(part, 0) + jnp.asarray(zero, part.dtype), value, neutral
-    )
-
-    def hop(position, subtotal):
-        longer = join(subtotal, jax.tree.map(lambda part: part[position], pieces))
-        return jax.tree.map(lambda new, old: jnp.where(position < mine, new, old), longer, subtotal)
-
-    return lax.fori_loop(0, count - 1, hop, subtotal)
 
 
 def kept_low(values):
@@ -64,8 +56,373 @@
     return (grad_weight, grad_offset, grad_ext)
 
 
-def combine(earlier, later):
-    return (earlier[0] * later[0], later[0][:, :, None, None] * earlier[1] + later[1])
+def scan_kernel(
+    peers, backward, s_ref, d_ref, out_ref,
+    part_s, part_d, carry_in, carry_out, back_out, back_in, send, recv,
+):
+    me = lax.axis_index("seq")
+    place = peers - 1 - me if backward else me
+    pairs = peers // 2
+    k, j = place // 2, place % 2
+    hh = part_s.shape[0]
+
+    def device(position):
+        return {"seq": peers - 1 - position if backward else position}
+
+    partner = device(place + 1 - 2 * j)
+    barrier = pltpu.get_barrier_semaphore()
+    for to in (partner, device((place + 2) % peers), device((place + peers - 2) % peers)):
+        pl.semaphore_signal(barrier, inc=1, device_id=to, device_id_type=MESH)
+    pl.semaphore_wait(barrier, 3)
+
+    def remote(source, target, slot, to):
+        return pltpu.make_async_remote_copy(
+            src_ref=source, dst_ref=target, send_sem=send.at[slot], recv_sem=recv.at[slot],
+            device_id=to, device_id_type=MESH,
+        )
+
+    theirs, mine = pl.ds((1 - j) * hh, hh), pl.ds(j * hh, hh)
+    give_s = remote(s_ref.at[theirs], part_s, 0, partner)
+    give_d = remote(d_ref.at[theirs], part_d, 1, partner)
+    give_s.start()
+    give_d.start()
+    give_s.wait()
+    give_d.wait()
+    early = j == 0
+    own_s, own_d = s_ref[mine], d_ref[mine]
+    s0 = jnp.where(early, own_s, part_s[...])
+    s1 = jnp.where(early, part_s[...], own_s)
+    d0 = jnp.where(early, own_d, part_d[...])
+    d1 = jnp.where(early, part_d[...], own_d)
+    onward = remote(carry_out, carry_in, 2, device((place + 2) % peers))
+
+    @pl.when(k == 0)
+    def _():
+        carry_in[...] = jnp.zeros_like(carry_in)
+
+    @pl.when(k > 0)
+    def _():
+        onward.wait_recv()
+
+    before = carry_in[...]
+    middle = d0 * before + s0
+
+    @pl.when(k < pairs - 1)
+    def _():
+        carry_out[...] = d1 * middle + s1
+        onward.start()
+
+    back_out[...] = jnp.where(early, middle, before)
+    back = remote(back_out, back_in, 3, partner)
+    back.start()
+    out_ref[mine] = jnp.where(early, before, middle)
+    back.wait()
+    out_ref[theirs] = back_in[...]
+
+    @pl.when(k < pairs - 1)
+    def _():
+        onward.wait_send()
+
+
+def state_scan(decay, state, backward):
+    heads, size, states = state.shape
+    hh = heads // 2
+    half = VMEM((hh, size, states), jnp.float32)
+    wide = jnp.broadcast_to(decay[:, None, None], (heads, 1, states))
+    return pl.pallas_call(
+        functools.partial(scan_kernel, lax.axis_size("seq"), backward),
+        out_shape=jax.ShapeDtypeStruct(state.shape, jnp.float32),
+        in_specs=[IN_VMEM] * 2,
+        out_specs=IN_VMEM,
+        scratch_shapes=[
+            half, VMEM((hh, 1, states), jnp.float32), half, half, half, half, DMA((4,)), DMA((4,)),
+        ],
+        compiler_params=pltpu.CompilerParams(
+            collective_id=2 if backward else 1, has_side_effects=True
+        ),
+        cost_estimate=pl.CostEstimate(
+            flops=10**7, bytes_accessed=5 * 10**7, transcendentals=0
+        ),
+        name="scan_back" if backward else "scan_ahead",
+    )(state, wide)
+
+
+def sums_kernel(
+    peers, groups, side_at,
+    rows_ref, right_ref, left_ref, cols_ref, minor_ref, back_ref, mix_ref, hidden_ref,
+    a_ref, b_ref, m_ref, g_ref, n_ref, o_ref,
+    s1a, s1b, r1a, r1b, s2a, s2b, r2a, r2b, rm1, sm, rm2, gs,
+    send1, recv1, send2, recv2, send_m, recv_m, send_g, recv_g,
+    got, n_sum, o_sum, send_h, recv_h,
+):
+    me, group = lax.axis_index("seq"), lax.axis_index("head")
+    pairs = peers // 2
+    k, j = me // 2, me % 2
+    partner = {"seq": me + 1 - 2 * j}
+    unroll = pairs <= 4
+    bf16 = jnp.bfloat16
+
+    def remote(source, target, here, there, to):
+        return pltpu.make_async_remote_copy(
+            src_ref=source, dst_ref=target, send_sem=here, recv_sem=there,
+            device_id=to, device_id_type=MESH,
+        )
+
+    def loop(count, body):
+        if unroll:
+            for t in range(count):
+                body(t)
+        else:
+            pl.loop(0, count)(body)
+
+    barrier = pltpu.get_barrier_semaphore()
+    pl.semaphore_signal(barrier, inc=1, device_id=partner, device_id_type=MESH)
+
+    def greet(t):
+        to = {"seq": 2 * ((k + 1 + t) % pairs) + j}
+        pl.semaphore_signal(barrier, inc=1, device_id=to, device_id_type=MESH)
+
+    loop(pairs - 1, greet)
+    for t in range(groups - 1):
+        to = {"head": (group + 1 + t) % groups}
+        pl.semaphore_signal(barrier, inc=1, device_id=to, device_id_type=MESH)
+    pl.semaphore_wait(barrier, pairs + groups - 1)
+
+    ways = [{"head": (group + 1 + t) % groups} for t in range(groups - 1)]
+    tokens = n_sum.shape[0]
+
+    def rows_of(owner):
+        return pl.ds(pl.multiple_of(owner * tokens, tokens), tokens)
+
+    def across(source, target, kind, t):
+        return remote(source, target, send_h.at[kind, t], recv_h.at[kind, t], ways[t])
+
+    partials = [
+        [
+            across(ref.at[rows_of((group + 1 + t) % groups)], got.at[kind, t], kind, t)
+            for t in range(groups - 1)
+        ]
+        for kind, ref in enumerate((back_ref, mix_ref))
+    ]
+    for copies in partials:
+        for copy in copies:
+            copy.start()
+
+    def piece(owner):
+        a = jnp.dot(rows_ref[owner], right_ref[...], preferred_element_type=jnp.float32)
+        b = jnp.dot(left_ref[...], cols_ref[owner], preferred_element_type=jnp.float32)
+        return a, b
+
+    def first(t):
+        return (
+            remote(s1a.at[t], r1a.at[t], send1.at[0, t], recv1.at[0, t], partner),
+            remote(s1b.at[t], r1b.at[t], send1.at[1, t], recv1.at[1, t], partner),
+        )
+
+    first_minor = remote(minor_ref, rm1, send_m.at[pairs], recv_m.at[pairs], partner)
+    first_minor.start()
+
+    def give(t):
+        a, b = piece(2 * ((k + 1 + t) % pairs) + 1 - j)
+        s1a[t] = a.astype(bf16)
+        s1b[t] = b.astype(bf16)
+        for copy in first(t):
+            copy.start()
+
+    loop(pairs, give)
+    first_minor.wait()
+    sm[...] = minor_ref[...] + rm1[...]
+
+    def second_minor(t):
+        to = {"seq": 2 * ((k + 1 + t) % pairs) + j}
+        return remote(sm, rm2.at[t], send_m.at[t], recv_m.at[t], to)
+
+    loop(pairs - 1, lambda t: second_minor(t).start())
+
+    own = rows_of(group)
+    for copy in partials[0]:
+        copy.wait()
+    summed = back_ref[own]
+    for t in range(groups - 1):
+        summed = summed + got[0, t]
+    n_sum[...] = summed
+    spread_n = [across(n_sum, n_ref.at[own], 2, t) for t in range(groups - 1)]
+    for copy in spread_n:
+        copy.start()
+    n_ref[own] = summed
+    for copy in partials[1]:
+        copy.wait()
+    summed = mix_ref[own]
+    for t in range(groups - 1):
+        summed = summed + got[1, t]
+    summed = (hidden_ref[own].astype(jnp.float32) + summed).astype(bf16)
+    o_sum[...] = summed
+    spread_o = [across(o_sum, o_ref.at[own], 3, t) for t in range(groups - 1)]
+    for copy in spread_o:
+        copy.start()
+    o_ref[own] = summed
+
+    def second(t):
+        to = {"seq": 2 * ((k + 1 + t) % pairs) + j}
+        return (
+            remote(s2a.at[t], r2a.at[t], send2.at[0, t], recv2.at[0, t], to),
+            remote(s2b.at[t], r2b.at[t], send2.at[1, t], recv2.at[1, t], to),
+        )
+
+    def join(t):
+        a, b = piece(2 * ((k + 1 + t) % pairs) + j)
+        for copy in first(t):
+            copy.wait()
+        return a + r1a[t].astype(jnp.float32), b + r1b[t].astype(jnp.float32)
+
+    def pass_on(t):
+        a, b = join(t)
+        s2a[t] = a.astype(bf16)
+        s2b[t] = b.astype(bf16)
+        for copy in second(t):
+            copy.start()
+
+    loop(pairs - 1, pass_on)
+    a, b = join(pairs - 1)
+    a_ref[...] = a
+    b_ref[...] = b
+
+    def collect(t):
+        for copy in second(t):
+            copy.wait()
+        a_ref[...] += r2a[t].astype(jnp.float32)
+        b_ref[...] += r2b[t].astype(jnp.float32)
+
+    loop(pairs - 1, collect)
+    gs[...] = a_ref[:, side_at:]
+    shares = [
+        remote(gs, g_ref.at[group], send_g.at[t], recv_g.at[t], {"head": (group + 1 + t) % groups})
+        for t in range(groups - 1)
+    ]
+    for copy in shares:
+        copy.start()
+    g_ref[group] = gs[...]
+
+    loop(pairs - 1, lambda t: second_minor(t).wait())
+
+    def ordered(q, total):
+        slot = (k - q + pairs - 1) % pairs
+        value = jnp.where(slot == pairs - 1, sm[...], rm2[jnp.minimum(slot, pairs - 2)])
+        return total + value
+
+    m_ref[...] = lax.fori_loop(0, pairs, ordered, jnp.zeros(m_ref.shape, jnp.float32))
+    for copy in shares + spread_n + spread_o:
+        copy.wait()
+
+
+def weight_sums_of(normed_in, right, normed_out, cotangent, minor, back, mix, hidden):
+    peers, groups = lax.axis_size("seq"), lax.axis_size("head")
+    pairs = peers // 2
+    length, width = normed_in.shape
+    part = width // peers
+    inner = normed_out.shape[1]
+    side = right.shape[1]
+    side_at = side - 128
+    rows = normed_in.T.reshape(peers, part, length)
+    cols = cotangent.reshape(length, peers, part).transpose(1, 0, 2)
+    low, full = jnp.bfloat16, jnp.float32
+    aa, bb = (part, side), (inner, part)
+    token_part = (length // groups, width)
+
+    def slots(count, shape, dtype):
+        return VMEM((count,) + shape, dtype)
+
+    return pl.pallas_call(
+        functools.partial(sums_kernel, peers, groups, side_at),
+        out_shape=(
+            jax.ShapeDtypeStruct(aa, full),
+            jax.ShapeDtypeStruct(bb, full),
+            jax.ShapeDtypeStruct(minor.shape, full),
+            jax.ShapeDtypeStruct((groups, part, 128), full),
+            jax.ShapeDtypeStruct(back.shape, full),
+            jax.ShapeDtypeStruct(hidden.shape, low),
+        ),
+        in_specs=[IN_VMEM] * 8,
+        out_specs=(IN_VMEM,) * 6,
+        scratch_shapes=[
+            slots(pairs, aa, low), slots(pairs, bb, low),
+            slots(pairs, aa, low), slots(pairs, bb, low),
+            slots(pairs - 1, aa, low), slots(pairs - 1, bb, low),
+            slots(pairs - 1, aa, low), slots(pairs - 1, bb, low),
+            VMEM(minor.shape, full), VMEM(minor.shape, full),
+            slots(pairs - 1, minor.shape, full),
+            VMEM((part, 128), full),
+            DMA((2, pairs)), DMA((2, pairs)), DMA((2, pairs)), DMA((2, pairs)),
+            DMA((pairs + 1,)), DMA((pairs + 1,)), DMA((groups,)), DMA((groups,)),
+            VMEM((2, groups - 1) + token_part, full), VMEM(token_part, full), VMEM(token_part, low),
+            DMA((4, groups - 1)), DMA((4, groups - 1)),
+        ],
+        compiler_params=pltpu.CompilerParams(
+            collective_id=3, has_side_effects=True, vmem_limit_bytes=48 * 2**20
+        ),
+        cost_estimate=pl.CostEstimate(
+            flops=10**9, bytes_accessed=2 * 10**8, transcendentals=0
+        ),
+        name="weight_sums",
+    )(rows, right, normed_out.T, cols, minor, back, mix, hidden)
+
+
+def head_sum_kernel(groups, x_ref, out_ref, got, total, send, recv):
+    me = lax.axis_index("head")
+    rows = total.shape[0]
+    barrier = pltpu.get_barrier_semaphore()
+    peers = [{"head": (me + 1 + t) % groups} for t in range(groups - 1)]
+    for to in peers:
+        pl.semaphore_signal(barrier, inc=1, device_id=to, device_id_type=MESH)
+    pl.semaphore_wait(barrier, groups - 1)
+
+    def remote(source, target, phase, t):
+        return pltpu.make_async_remote_copy(
+            src_ref=source, dst_ref=target, send_sem=send.at[phase, t], recv_sem=recv.at[phase, t],
+            device_id=peers[t], device_id_type=MESH,
+        )
+
+    def rows_of(owner):
+        return pl.ds(pl.multiple_of(owner * rows, rows), rows)
+
+    gives = [
+        remote(x_ref.at[rows_of((me + 1 + t) % groups)], got.at[t], 0, t)
+        for t in range(groups - 1)
+    ]
+    for copy in gives:
+        copy.start()
+    for copy in gives:
+        copy.wait()
+    summed = x_ref[rows_of(me)]
+    for t in range(groups - 1):
+        summed = summed + got[t]
+    total[...] = summed
+    shares = [remote(total, out_ref.at[rows_of(me)], 1, t) for t in range(groups - 1)]
+    for copy in shares:
+        copy.start()
+    out_ref[rows_of(me)] = summed
+    for copy in shares:
+        copy.wait()
+
+
+def head_sum(value):
+    groups = lax.axis_size("head")
+    part = (value.shape[0] // groups, value.shape[1])
+    return pl.pallas_call(
+        functools.partial(head_sum_kernel, groups),
+        out_shape=jax.ShapeDtypeStruct(value.shape, jnp.float32),
+        in_specs=[IN_VMEM],
+        out_specs=IN_VMEM,
+        scratch_shapes=[
+            VMEM((groups - 1,) + part, jnp.float32), VMEM(part, jnp.float32),
+            DMA((2, groups - 1)), DMA((2, groups - 1)),
+        ],
+        compiler_params=pltpu.CompilerParams(collective_id=4, has_side_effects=True),
+        cost_estimate=pl.CostEstimate(
+            flops=10**6, bytes_accessed=3 * 10**7, transcendentals=0
+        ),
+        name="head_sum",
+    )(value)
 
 
 def on_device(
@@ -123,10 +480,7 @@
     tail_w = tail_exp * deltas
     weighted_x = tail_w[..., None] * x_heads
     local_state = jnp.einsum("sthp,stn->shpn", weighted_x, b_mat, precision=HIGHEST)
-    empty_state = jnp.zeros_like(local_state)
-    incoming = entering(
-        (block_decay, local_state), "seq", combine, (jnp.ones_like(block_decay), empty_state), False
-    )[1]
+    incoming = state_scan(block_decay[0], local_state[0], False)[None]
     scores = jnp.einsum("stn,sun->stu", c_mat, b_mat, precision=HIGHEST)
     row_ids = lax.broadcasted_iota(jnp.int32, (length, length), 0)
     column_ids = lax.broadcasted_iota(jnp.int32, (length, length), 1)
@@ -142,19 +496,15 @@
     flat_ssd = ssd_out.reshape(seq_count, length, inner_dev)
     gate_act = jax.nn.silu(gating)
     gated = flat_ssd * gate_act
-    squares = lax.psum(jnp.sum(gated * gated, axis=-1), "head")
+    grad_normed = jnp.einsum("std,ed->ste", cotangent, w_out, preferred_element_type=jnp.float32)
+    scaled_out = grad_normed * gate_gain
+    squares, dotted = lax.psum(
+        jnp.stack([jnp.sum(gated * gated, axis=-1), jnp.sum(scaled_out * gated, axis=-1)]), "head"
+    )
     gate_rstd = lax.rsqrt(squares / full_inner + EPSILON)[..., None]
     normed_out = (gated * gate_rstd * gate_gain).astype(jnp.bfloat16)
     partial_value = jnp.einsum("ste,ed->std", normed_out, w_out, preferred_element_type=jnp.float32)
-    mixed = lax.psum(partial_value, "head")
-    output = (residual + mixed).astype(jnp.bfloat16)
-    grad_w_out = jnp.einsum(
-        "ste,std->ed", normed_out, cotangent, preferred_element_type=jnp.float32
-    )
-    grad_normed = jnp.einsum("std,ed->ste", cotangent, w_out, preferred_element_type=jnp.float32)
     grad_gate_gain = jnp.sum(grad_normed * gated * gate_rstd, axis=(0, 1))
-    scaled_out = grad_normed * gate_gain
-    dotted = lax.psum(jnp.sum(scaled_out * gated, axis=-1), "head")
     grad_gated = gate_rstd * scaled_out - gated * gate_rstd**3 * (dotted / full_inner)[..., None]
     grad_ssd = (grad_gated * gate_act).reshape(seq_count, length, head_count, head_size)
     grad_gating = grad_gated * flat_ssd * silu_slope(gating)
@@ -164,13 +514,7 @@
     grad_cum = jnp.sum(grad_ssd * outside, axis=-1)
     state_grad_local = jnp.einsum("sthp,stn->shpn", grad_from, c_mat, precision=HIGHEST)
     grad_c = jnp.einsum("sthp,shpn->stn", grad_from, incoming, precision=HIGHEST)
-    after = entering(
-        (block_decay, state_grad_local),
-        "seq",
-        combine,
-        (jnp.ones_like(block_decay), empty_state),
-        True,
-    )[1]
+    after = state_scan(block_decay[0], state_grad_local[0], True)[None]
     grad_last = jnp.sum(after * incoming, axis=(2, 3)) * block_decay
     grad_weighted = jnp.einsum("shpn,stn->sthp", after, b_mat, precision=HIGHEST)
     grad_b = jnp.einsum("sthp,shpn->stn", weighted_x, after, precision=HIGHEST)
@@ -193,7 +537,7 @@
     grad_u = (grad_deltas + grad_log_decay * rates) * jax.nn.sigmoid(dt_raw + dt_bias)
     grad_dt_bias = jnp.sum(grad_u, axis=(0, 1))
     grad_dt_raw = grad_u.astype(jnp.bfloat16)
-    grad_bc_post = lax.psum(jnp.concatenate([grad_b, grad_c], -1), "head")
+    grad_bc_post = head_sum(jnp.concatenate([grad_b[0], grad_c[0]], -1))[None]
     grad_pre_x = grad_x.reshape(seq_count, length, inner_dev) * silu_slope(pre_x)
     grad_pre_bc = grad_bc_post * silu_slope(pre_bc)
     grad_conv_x_w, grad_conv_x_b, grad_ext_x = conv_reverse(ext_x, conv_x_w, grad_pre_x, length)
@@ -206,24 +550,52 @@
     tail_pad = ((0, 0), (length - conv_reach, 0), (0, 0))
     grad_conv_in = grad_ext_x[:, conv_reach:] + jnp.pad(sent_x, tail_pad)
     grad_bc_in = (grad_ext_bc[:, conv_reach:] + jnp.pad(sent_bc, tail_pad)).astype(jnp.bfloat16)
-    grad_projected = jnp.stack([grad_gating, grad_conv_in], 2).astype(jnp.bfloat16)
-    grad_w_zx = jnp.einsum(
-        "std,stke->dke", normed_in, grad_projected, preferred_element_type=jnp.float32
-    )
-    grad_w_bc = jnp.einsum("std,stn->dn", normed_in, grad_bc_in, preferred_element_type=jnp.float32)
-    grad_w_dt = jnp.einsum(
-        "std,sth->dh", normed_in, grad_dt_raw, preferred_element_type=jnp.float32
-    )
+    grad_projected = jnp.concatenate([grad_gating, grad_conv_in], -1).astype(jnp.bfloat16)
     head_part = jnp.einsum(
-        "stke,dke->std", grad_projected, w_zx, preferred_element_type=jnp.float32
+        "ste,de->std",
+        grad_projected,
+        w_zx.reshape(w_zx.shape[0], 2 * inner_dev),
+        preferred_element_type=jnp.float32,
     )
     head_part = head_part + jnp.einsum(
         "sth,dh->std", grad_dt_raw, w_dt, preferred_element_type=jnp.float32
     )
-    grad_normed_in = lax.psum(head_part, "head")
-    grad_normed_in = grad_normed_in + jnp.einsum(
-        "stn,dn->std", grad_bc_in, w_bc, preferred_element_type=jnp.float32
-    )
+    groups = lax.axis_size("head")
+    share = w_bc.shape[1] // groups
+    group_at = lax.axis_index("head") * share
+    group_bc = lax.dynamic_slice_in_dim(grad_bc_in, group_at, share, axis=2)
+    head_part = head_part + jnp.einsum(
+        "stn,dn->std",
+        group_bc,
+        lax.dynamic_slice_in_dim(w_bc, group_at, share, axis=1),
+        preferred_element_type=jnp.float32,
+    )
+    side = jnp.concatenate([group_bc[0], grad_dt_raw[0]], -1)
+    spare = jnp.zeros((length, 128 - share - head_count), jnp.bfloat16)
+    right = jnp.concatenate([grad_projected[0], side, spare], -1)
+    minor = (
+        grad_conv_x_w,
+        grad_conv_x_b,
+        grad_conv_bc_w,
+        grad_conv_bc_b,
+        grad_gate_gain,
+        grad_dt_bias,
+        grad_a_log,
+        grad_d_skip,
+    )
+    flat = jnp.concatenate([part.reshape(-1) for part in minor])
+    flat = jnp.pad(flat, (0, -flat.size % 1024)).reshape(-1, 128)
+    side_sum, out_sum, minor_sum, shared, back_sum, output = weight_sums_of(
+        normed_in[0],
+        right,
+        normed_out[0],
+        cotangent[0],
+        flat,
+        head_part[0],
+        partial_value[0],
+        hidden[0],
+    )
+    grad_normed_in = back_sum[None]
     grad_pre_gain = jnp.sum(grad_normed_in * residual * in_rstd, axis=(0, 1))
     scaled_in = grad_normed_in * pre_gain
     grad_hidden = (
@@ -231,42 +603,30 @@
         + in_rstd * scaled_in
         - residual * in_rstd**3 * jnp.mean(scaled_in * residual, axis=-1, keepdims=True)
     )
-    weight_sums = (
-        lax.psum_scatter(grad_w_zx, "seq", scatter_dimension=0, tiled=True),
-        lax.psum_scatter(grad_w_bc, "seq", scatter_dimension=0, tiled=True),
-        lax.psum_scatter(grad_w_dt, "seq", scatter_dimension=0, tiled=True),
-        lax.psum_scatter(grad_w_out, "seq", scatter_dimension=1, tiled=True),
-    )
-    minor_sums = lax.psum(
-        (
-            grad_pre_gain,
-            grad_conv_x_w,
-            grad_conv_x_b,
-            grad_conv_bc_w,
-            grad_conv_bc_b,
-            grad_dt_bias,
-            grad_a_log,
-            grad_d_skip,
-            grad_gate_gain,
-        ),
-        "seq",
-    )
+    line, minor_sums, at = minor_sum.reshape(-1), [], 0
+    for part in minor:
+        minor_sums.append(line[at : at + part.size].reshape(part.shape))
+        at += part.size
+    rows_here = side_sum.shape[0]
+    sum_zx = side_sum[:, : 2 * inner_dev].reshape(rows_here, 2, inner_dev)
+    sum_dt = side_sum[:, 2 * inner_dev + share : 2 * inner_dev + share + head_count]
+    sum_bc = shared[:, :, :share].transpose(1, 0, 2).reshape(rows_here, groups * share)
     return (
-        output,
+        output[None],
         grad_hidden,
+        lax.psum(grad_pre_gain, "seq"),
+        sum_zx,
+        sum_bc,
+        sum_dt,
         minor_sums[0],
-        weight_sums[0],
-        weight_sums[1],
-        weight_sums[2],
         minor_sums[1],
         minor_sums[2],
         minor_sums[3],
-        minor_sums[4],
         minor_sums[5],
         minor_sums[6],
         minor_sums[7],
-        minor_sums[8],
-        weight_sums[3],
+        minor_sums[4],
+        out_sum,
     )
 
 

time: 568 us -> 275 us (0.48)
  waiting for transfers between devices: 339 us -> 7.47 us
  Pallas kernels: 0 us -> 121 us
  blocking collectives: 69.5 us -> 34.4 us
  matrix products: 46.3 us -> 31.3 us
  between operations: 15.2 us -> 1.85 us
  other arithmetic: 43.3 us -> 34.4 us
  local copies, waits for them, and re-layouts: 40 us -> 31.9 us
    reduce_scatter x4 -> x0, waiting for transfers between devices: 235 us -> none  [the longest x1 72.1 us: on_device(): lax.psum_scatter(grad_w_out, 'seq', scatter_dimension=1, tiled=True)]
    pallas_call x0 -> x4, Pallas kernels: none -> 121 us  [the longest x1 63.3 us: weight_sums_of(): pl.pallas_call(functools.partial(sums_kernel, peers, groups, side_at), ou...]
    all_gather x2 -> x0, waiting for transfers between devices: 51.3 us -> none  [entering(): pieces = jax.tree.map(lambda part: lax.all_gather(part, axis), value)]
    psum x1 -> x0, waiting for transfers between devices: 47 us -> none  [on_device(): mixed = lax.psum(partial_value, 'head')]
    mul x22 -> x0, local copies, waits for them, and re-layouts: 19.2 us -> none  [the longest x14 9.04 us: combine(): later[0][:, :, None, None] * earlier[1] + later[1]]
    all_gather x1 -> x0, blocking collectives: 18.9 us -> none  [entering(): pieces = jax.tree.map(lambda part: lax.all_gather(part, axis), value)]
    psum x3 -> x2, blocking collectives: 50.6 us -> 34.4 us  [the longest x1 28.7 us: on_device(): lax.psum(grad_pre_gain, 'seq')]
    select_n x14 -> x0, other arithmetic: 14.7 us -> none  [hop(): jnp.where(position < mine, new, old)]
  transfers between devices with their start and end apart: 11 -> 4, of which waited for: 9 -> 2; matrix products, arithmetic and copies ran while one was open for 9% -> 10% of each run, Pallas kernels for 0% -> 0%
where the time goes in v1:
time: 275 us; the launch traced here: 274 us
  Pallas kernels  121 us (44%)
  other arithmetic  34.4 us (13%)
  blocking collectives  34.4 us (13%)
  local copies, waits for them, and re-layouts  31.9 us (12%)
  matrix products  31.3 us (11%)
  starting transfers between devices  11.9 us (4%)
  waiting for transfers between devices  7.47 us (3%)
    pallas_call x1, Pallas kernels, weight_sums_of(): pl.pallas_call(functools.partial(sums_kernel, peers, groups, side_at), ou...  63.3 us
    pallas_call x2, Pallas kernels, state_scan(): pl.pallas_call(functools.partial(scan_kernel, lax.axis_size('seq'), backw...  46.3 us
    psum x1, blocking collectives, on_device(): lax.psum(grad_pre_gain, 'seq')  28.7 us
    ppermute x4, starting transfers between devices, from_behind(): return lax.ppermute(value, axis, pairs)  11.9 us
    unnamed x185, local copies, waits for them, and re-layouts  11.4 us
    pallas_call x1, Pallas kernels, head_sum(): pl.pallas_call(functools.partial(head_sum_kernel, groups), out_shape=jax....  11.2 us
    ppermute x4, waiting for transfers between devices, from_behind(): return lax.ppermute(value, axis, pairs)  7.47 us
    psum x1, blocking collectives, on_device(): lax.psum(jnp.stack([jnp.sum(gated * gated, axis=-1), jnp.sum(scaled_out *...  5.67 us
  transfers between devices with their start and end apart: 4, of which 2 were waited for; matrix products, arithmetic and copies ran while one was open for 10% of the time, Pallas kernels for 0%

profile of v1, /device:TPU:0, one launch (start us, length us, event | category | flops | bytes accessed | tf_op | source)
XLA Modules:
  0.0 273.9 jit_solution(9012456193466184025)
XLA Ops:
  0.7 1.3 fusion.20
  2.6 1.6 fusion.19
  4.8 5.6 %collective-permute-start.1 = (bf16[1,3,256]{2,1,0:T(4,128)(2,1)}, bf16[1,3,256]{2,1,0:T(4,128)(2,1)}, u32[]{:S(2)}, u32[]{:S(2)}) collective-permute-start(bf16[1,3,256]{2,1,0:T(4,128)(2,1)} %slice.229), channel_id=1, source_target_pairs={{0,4},{4,8},{8,12},{12,16},{16,20},{20,24},{24,28},{1,5},{5,9},{9,... | collective-permute-start | bytes 4616 | tf_op jit(solution)/shard_map/ppermute | solution.py:22
  10.4 2.6 fusion.8
  13.0 0.9 slice.224
  13.9 3.5 %collective-permute-start = (bf16[1,3,512]{1,2,0:T(8,128)(2,1)}, bf16[1,3,512]{1,2,0:T(8,128)(2,1)}, u32[]{:S(2)}, u32[]{:S(2)}) collective-permute-start(bf16[1,3,512]{1,2,0:T(8,128)(2,1)} %slice.224), channel_id=1, source_target_pairs={{0,4},{4,8},{8,12},{12,16},{16,20},{20,24},{24,28},{1,5},{5,9},{9,... | collective-permute-start | bytes 9224 | tf_op jit(solution)/shard_map/ppermute | solution.py:22
  20.6 1.7 fusion.96
  22.3 1.4 fusion.106
  23.7 1.4 fusion.105
  25.3 1.4 bitcast_multiply_fusion.16
  27.9 2.0 copy.62
  29.9 1.0 copy.73
  30.9 2.0 copy.74
  33.0 3.5 %copy.90 = bf16[128,8,2,512]{3,1,2,0:T(8,128)(2,1)} copy(bf16[128,8,2,512]{3,2,1,0:T(2,128)(2,1)} %bitcast.325) | data formatting | bytes 4194304
  36.5 0.7 maximum_convert_fusion.1
  37.3 0.9 multiply_convert_fusion.2
  38.2 0.9 fusion.74
  39.1 1.1 maximum_convert_fusion
  40.3 1.6 multiply_convert_fusion.1
  41.9 0.8 convert_element_type.118
  42.8 0.8 copy-done.10
  43.6 1.1 fusion.68.s_ref
  45.3 11.2 %scan_ahead.1 = f32[8,64,128]{2,1,0:T(8,128)} custom-call(f32[8,64,128]{2,1,0:T(8,128)} %fusion.68.s_ref, f32[8,1,128]{2,1,0:T(1,128)} %broadcast_in_dim.36.d_ref), custom_call_target="tpu_custom_call" | custom-call | flops 10000000 | bytes 50000000 | tf_op jit(solution)/shard_map/scan_ahead/pallas_call | solution.py:132
  56.5 1.3 convolution_multiply_fusion
  57.9 3.2 %multiply_reduce_fusion.8 = (f32[256]{0:T(256)S(1)}, f32[1,256,8,64]{1,3,2,0:T(8,128)S(1)}) fusion(f32[1,256,8,64]{1,3,2,0:T(8,128)S(1)} %bitcast.324, f32[1,256,8,64]{1,3,2,0:T(8,128)} %bitcast.326, f32[8]{0:T(128)} %param.29, f32[256,8,64]{0,2,1:T(8,128)S(1)} %convolution_multiply_fusion, bf16[256,8,64]{0,2,1:T(8,128)(2,1)S(1)} %bitcast.322, ...), kind=kOutput, calls=%fused_computation.97 | convolution fusion | flops 406585088 | bytes 2704416 | tf_op jit(solution)/shard_map/stuh,suhp->sthp/dot_general | solution.py:491
  61.2 1.3 multiply_reduce_fusion.7
  62.5 5.7 %psum.14 = f32[2,1,256]{2,1,0:T(1,128)S(1)} all-reduce(f32[2,1,256]{2,1,0:T(1,128)S(1)} %pad_maximum_fusion.1), channel_id=1, replica_groups=mesh['seq'=8,'head'=4] {'head'}, use_global_device_ids=true, to_apply=%region_5.6 | all-reduce | flops 512 | bytes 4096 | tf_op jit(solution)/shard_map/psum | solution.py:501
  68.3 3.2 %multiply_reduce_fusion = (f32[512]{0:T(512)}, bf16[256,512]{0,1:T(8,128)(2,1)}, bf16[512,256]{1,0:T(8,128)(2,1)S(1)}) fusion(f32[256,512]{0,1:T(8,128)} %get-tuple-element.151, f32[256,512]{0,1:T(8,128)S(1)} %get-tuple-element.109, f32[256]{0:T(256)S(1)} %bitcast.335, f32[1,256,2,512]{1,3,2,0:T(8,128)} %copy-done.17, f32[1,256,8,64]{1,3,2,0:T(8,128)} %copy-done.30, ...), kind=kLoop, calls=%fused_computation.87 | loop fusion | flops 2752000 | bytes 2628608 | tf_op jit(solution)/shard_map/reduce_sum | solution.py:507
  71.5 2.1 fusion.45
  73.6 0.7 multiply_reduce_fusion.5
  74.3 1.7 convolution_bitcast_fusion
  76.0 1.1 fusion.70.s_ref
  77.1 35.1 %scan_back.1 = f32[8,64,128]{2,1,0:T(8,128)} custom-call(f32[8,64,128]{2,1,0:T(8,128)} %fusion.70.s_ref, f32[8,1,128]{2,1,0:T(1,128)} %broadcast_in_dim.36.d_ref), custom_call_target="tpu_custom_call" | custom-call | flops 10000000 | bytes 50000000 | tf_op jit(solution)/shard_map/scan_back/pallas_call | solution.py:132
  112.2 2.2 convolution_bitcast_fusion.1
  114.4 1.7 multiply_reduce_fusion.13
  116.0 2.6 fusion.93.mix_ref
  118.7 3.2 %fusion.15 = (f32[256,8]{0,1:T(8,128)}, f32[256,8]{0,1:T(8,128)}, f32[256,8]{0,1:T(8,128)}, f32[256,256]{1,0:T(8,128)S(1)}) fusion(f32[256,256]{1,0:T(8,128)S(1)} %copy-done.31, f32[256,8]{0,1:T(8,128)S(1)} %copy-done.62, f32[256,8]{0,1:T(8,128)S(1)} %copy-done.66, pred[256,256]{1,0:T(8,128)(4,1)S(1)} %copy-done.38, bf16[256,8,64]{0,2,1:T(8,128)(2,1)S(1)} %bitcast.323, ...), kind=kOutput, calls=%fused_computation.25 | convolution fusion | flops 409921536 | bytes 1417216 | tf_op jit(solution)/shard_map/sthp,suhp->stuh/dot_general | solution.py:526
  122.6 0.7 pad_maximum_fusion.x_ref
  123.3 11.2 %head_sum.1 = f32[256,256]{1,0:T(8,128)} custom-call(f32[256,256]{1,0:T(8,128)} %pad_maximum_fusion.x_ref), custom_call_target="tpu_custom_call" | custom-call | flops 1000000 | bytes 30000000 | tf_op jit(solution)/shard_map/head_sum/pallas_call | solution.py:411
  134.5 1.8 multiply_reduce_fusion.12
  136.4 0.9 broadcast_multiply_fusion.7
  137.9 0.8 pad_add_fusion.1
  139.2 2.0 fusion.16
  141.2 0.9 multiply_reduce_fusion.4
  144.4 0.7 copy.71
  147.6 0.7 constant_dynamic-update-slice_fusion.2
  148.3 1.3 collective-permute-start.3
  149.6 0.7 concatenate.49
  150.4 1.5 collective-permute-start.2
  151.9 1.9 collective-permute-done.3
  153.9 2.3 fusion.60
  156.3 5.6 %collective-permute-done.2 = f32[1,3,512]{1,2,0:T(8,128)S(1)} collective-permute-done((f32[1,3,512]{1,2,0:T(8,128)S(1)}, f32[1,3,512]{1,2,0:T(8,128)S(1)}, u32[]{:S(2)}, u32[]{:S(2)}) %collective-permute-start.2) | collective-permute-done | bytes 6176 | tf_op jit(solution)/shard_map/ppermute | solution.py:22
  161.9 1.0 constant_dynamic-update-slice_fusion.1
  164.7 1.4 copy.76.right_ref
  166.1 2.6 fusion.41
  169.9 63.3 %weight_sums.1 = (f32[128,1152]{1,0:T(8,128)S(1)}, f32[512,128]{1,0:T(8,128)S(1)}, f32[40,128]{1,0:T(8,128)S(1)}, f32[4,128,128]{2,1,0:T(8,128)S(1)}, f32[256,10...) custom-call(bf16[8,128,256]{2,1,0:T(8,128)(2,1)S(1)} %bitcast.311, bf16[256,1152]{1,0:T(8,128)(2,1)S(1)} %copy.76.right_ref, ...), custom_call_target="tpu_custom_call" | custom-call | flops 1000000000 | bytes 200000000 | tf_op jit(solution)/shard_map/weight_sums/pallas_call | solution.py:335
  236.9 28.7 %psum.15 = f32[1024]{0:T(1024)} all-reduce(f32[1024]{0:T(1024)S(1)} %get-tuple-element.88), channel_id=1, replica_groups=mesh['seq'=8,'head'=4] {'seq'}, use_global_device_ids=true, to_apply=%region_33.34 | all-reduce | flops 1024 | bytes 8192 | tf_op jit(solution)/shard_map/psum | solution.py:617
  266.2 1.2 reshape.759
  267.5 0.7 slice_bitcast_fusion
  268.2 1.1 copy.77
  269.3 0.8 copy.78
  270.0 2.4 fusion.24
  272.4 0.8 copy.102
  273.2 0.7 copy.103
  (245 shorter events, 20.2 us)
Async XLA Ops:
  0.6 60.5 %copy-start = (bf16[512,1024]{1,0:T(8,128)(2,1)S(1)}, bf16[512,1024]{1,0:T(8,128)(2,1)}, u32[]{:S(2)}) copy-start(bf16[512,1024]{1,0:T(8,128)(2,1)} %param.31) | copy-start | bytes 3145732
  0.7 9.7 %copy-start.1 = (bf16[1,256,1024]{2,1,0:T(8,128)(2,1)S(1)}, bf16[1,256,1024]{2,1,0:T(8,128)(2,1)}, u32[]{:S(2)}) copy-start(bf16[1,256,1024]{2,1,0:T(8,128)(2,1)} %param.17) | copy-start | bytes 1572868
  0.7 9.7 %copy-start.40 = (f32[1024]{0:T(1024)S(1)}, f32[1024]{0:T(1024)}, u32[]{:S(2)}) copy-start(f32[1024]{0:T(1024)} %param.19) | copy-start | bytes 12292
  2.6 14.9 %copy-start.53 = (f32[256]{0:T(256)}, f32[256]{0:T(256)S(1)}, u32[]{:S(2)}) copy-start(f32[256]{0:T(256)S(1)} %get-tuple-element.150) | copy-start | bytes 3076
  4.8 12.7 %copy-start.86 = (f32[8]{0:T(128)S(1)}, f32[8]{0:T(128)}, u32[]{:S(2)}) copy-start(f32[8]{0:T(128)} %param.28) | copy-start | bytes 100
  4.8 12.7 %copy-start.55 = (bf16[1024,8]{0,1:T(8,128)(2,1)S(1)}, bf16[1024,8]{0,1:T(8,128)(2,1)}, u32[]{:S(2)}) copy-start(bf16[1024,8]{0,1:T(8,128)(2,1)} %param.22) | copy-start | bytes 49156
  4.8 12.7 %copy-start.84 = (f32[8]{0:T(128)S(1)}, f32[8]{0:T(128)}, u32[]{:S(2)}) copy-start(f32[8]{0:T(128)} %param.27) | copy-start | bytes 100
  4.8 31.7 %collective-permute-start.1 = (bf16[1,3,256]{2,1,0:T(4,128)(2,1)}, bf16[1,3,256]{2,1,0:T(4,128)(2,1)}, u32[]{:S(2)}, u32[]{:S(2)}) collective-permute-start(bf16[1,3,256]{2,1,0:T(4,128)(2,1)} %slice.229), channel_id=1, source_target_pairs={{0,4},{4,8},{8,12},{12,16},{16,20},{20,24},{24,28},{1,5},{5,9},{9,... | collective-permute-start | bytes 4616 | tf_op jit(solution)/shard_map/ppermute | solution.py:22
  13.0 17.0 %copy-start.17 = (f32[1,256,2,512]{1,3,2,0:T(8,128)}, f32[1,256,2,512]{1,3,2,0:T(8,128)S(1)}, u32[]{:S(2)}) copy-start(f32[1,256,2,512]{1,3,2,0:T(8,128)S(1)} %fusion.8) | copy-start | bytes 3145732
  13.9 25.2 %collective-permute-start = (bf16[1,3,512]{1,2,0:T(8,128)(2,1)}, bf16[1,3,512]{1,2,0:T(8,128)(2,1)}, u32[]{:S(2)}, u32[]{:S(2)}) collective-permute-start(bf16[1,3,512]{1,2,0:T(8,128)(2,1)} %slice.224), channel_id=1, source_target_pairs={{0,4},{4,8},{8,12},{12,16},{16,20},{20,24},{24,28},{1,5},{5,9},{9,... | collective-permute-start | bytes 9224 | tf_op jit(solution)/shard_map/ppermute | solution.py:22
  17.5 12.4 %copy-start.22 = (bf16[1,256,1024]{2,1,0:T(8,128)(2,1)S(1)}, bf16[1,256,1024]{2,1,0:T(8,128)(2,1)}, u32[]{:S(2)}) copy-start(bf16[1,256,1024]{2,1,0:T(8,128)(2,1)} %param.18) | copy-start | bytes 1572868
  23.7 13.6 %copy-start.57 = (f32[1,256]{1,0:T(1,128)}, f32[1,256]{1,0:T(1,128)S(1)}, u32[]{:S(2)}) copy-start(f32[1,256]{1,0:T(1,128)S(1)} %get-tuple-element.143) | copy-start | bytes 3076
  23.7 13.6 %copy-start.58 = (f32[1,256]{1,0:T(1,128)}, f32[1,256]{1,0:T(1,128)S(1)}, u32[]{:S(2)}) copy-start(f32[1,256]{1,0:T(1,128)S(1)} %get-tuple-element.144) | copy-start | bytes 3076
  33.0 4.3 %copy-start.59 = (f32[1,256]{1,0:T(1,128)S(1)}, f32[1,256]{1,0:T(1,128)}, u32[]{:S(2)}) copy-start(f32[1,256]{1,0:T(1,128)} %get-tuple-element.145) | copy-start | bytes 3076
  33.0 4.4 %copy-start.60 = (f32[1,256]{1,0:T(1,128)S(1)}, f32[1,256]{1,0:T(1,128)}, u32[]{:S(2)}) copy-start(f32[1,256]{1,0:T(1,128)} %get-tuple-element.146) | copy-start | bytes 3076
  33.0 4.4 %copy-start.82 = (f32[256]{0:T(256)S(1)}, f32[256]{0:T(256)}, u32[]{:S(2)}) copy-start(f32[256]{0:T(256)} %param.26) | copy-start | bytes 3076
  36.5 3.7 %copy-start.44 = (f32[1,512]{1,0:T(1,128)S(1)}, f32[1,512]{1,0:T(1,128)}, u32[]{:S(2)}) copy-start(f32[1,512]{1,0:T(1,128)} %get-tuple-element.139) | copy-start | bytes 6148
  36.5 3.7 %copy-start.46 = (f32[1,512]{1,0:T(1,128)S(1)}, f32[1,512]{1,0:T(1,128)}, u32[]{:S(2)}) copy-start(f32[1,512]{1,0:T(1,128)} %get-tuple-element.140) | copy-start | bytes 6148
  36.5 3.7 %copy-start.48 = (f32[1,512]{1,0:T(1,128)S(1)}, f32[1,512]{1,0:T(1,128)}, u32[]{:S(2)}) copy-start(f32[1,512]{1,0:T(1,128)} %get-tuple-element.141) | copy-start | bytes 6148
  36.5 3.7 %copy-start.50 = (f32[1,512]{1,0:T(1,128)S(1)}, f32[1,512]{1,0:T(1,128)}, u32[]{:S(2)}) copy-start(f32[1,512]{1,0:T(1,128)} %get-tuple-element.142) | copy-start | bytes 6148
  36.5 3.7 %copy-start.79 = (f32[512]{0:T(512)S(1)}, f32[512]{0:T(512)}, u32[]{:S(2)}) copy-start(f32[512]{0:T(512)} %param.24) | copy-start | bytes 6148
  40.2 2.5 copy-start.34
  40.3 4.4 %copy-start.83 = (f32[8]{0:T(128)S(1)}, f32[8]{0:T(128)}, u32[]{:S(2)}) copy-start(f32[8]{0:T(128)} %exp.87) | copy-start | bytes 100
  41.9 19.3 %copy-start.12 = (bf16[1,256,512]{1,2,0:T(8,128)(2,1)}, bf16[1,256,512]{1,2,0:T(8,128)(2,1)S(1)}, u32[]{:S(2)}) copy-start(bf16[1,256,512]{1,2,0:T(8,128)(2,1)S(1)} %get-tuple-element.114) | copy-start | bytes 786436
  41.9 16.0 %slice-start = ((f32[1,256,2,512]{1,3,2,0:T(8,128)}), f32[1,256,1,512]{1,3,2,0:T(8,128)S(1)}, s32[]{:S(2)}) async-start(f32[1,256,2,512]{1,3,2,0:T(8,128)} %copy-done.17), calls=%async_computation | async-start | bytes 1048576 | tf_op jit(solution)/shard_map/slice | solution.py:456
  57.9 3.3 %copy-start.25 = (f32[256,8,64]{0,2,1:T(8,128)}, f32[256,8,64]{0,2,1:T(8,128)S(1)}, u32[]{:S(2)}) copy-start(f32[256,8,64]{0,2,1:T(8,128)S(1)} %convolution_multiply_fusion) | copy-start | bytes 1572868
  57.9 3.3 %copy-start.18 = (f32[1,256,2,512]{1,3,2,0:T(8,128)S(1)}, f32[1,256,2,512]{1,3,2,0:T(8,128)}, u32[]{:S(2)}) copy-start(f32[1,256,2,512]{1,3,2,0:T(8,128)} %copy-done.17) | copy-start | bytes 3145732
  57.9 3.3 %copy-start.23 = (bf16[1,256,1024]{2,1,0:T(8,128)(2,1)S(1)}, bf16[1,256,1024]{2,1,0:T(8,128)(2,1)}, u32[]{:S(2)}) copy-start(bf16[1,256,1024]{2,1,0:T(8,128)(2,1)} %param.18) | copy-start | bytes 1572868
  57.9 3.3 %copy-start.52 = (f32[512]{0:T(512)S(1)}, f32[512]{0:T(512)}, u32[]{:S(2)}) copy-start(f32[512]{0:T(512)} %param.30) | copy-start | bytes 6148
  62.5 5.7 %copy-start.11 = (f32[256,512]{0,1:T(8,128)}, f32[256,512]{0,1:T(8,128)S(1)}, u32[]{:S(2)}) copy-start(f32[256,512]{0,1:T(8,128)S(1)} %get-tuple-element.109) | copy-start | bytes 1572868
  68.2 3.2 %copy-start.19 = (f32[1,256,2,512]{1,3,2,0:T(8,128)S(1)}, f32[1,256,2,512]{1,3,2,0:T(8,128)}, u32[]{:S(2)}) copy-start(f32[1,256,2,512]{1,3,2,0:T(8,128)} %copy-done.17) | copy-start | bytes 3145732
  68.2 3.2 %copy-start.27 = (f32[256,512]{0,1:T(8,128)S(1)}, f32[256,512]{0,1:T(8,128)}, u32[]{:S(2)}) copy-start(f32[256,512]{0,1:T(8,128)} %get-tuple-element.151) | copy-start | bytes 1572868
  68.2 5.3 %copy-start.43 = (f32[1,1,256]{2,1,0:T(1,128)}, f32[1,1,256]{2,1,0:T(1,128)S(1)}, u32[]{:S(2)}) copy-start(f32[1,1,256]{2,1,0:T(1,128)S(1)} %get-tuple-element.147) | copy-start | bytes 3076
  68.3 5.3 %copy-start.26 = (f32[256,8,64]{0,2,1:T(8,128)S(1)}, f32[256,8,64]{0,2,1:T(8,128)}, u32[]{:S(2)}) copy-start(f32[256,8,64]{0,2,1:T(8,128)} %copy-done.25) | copy-start | bytes 1572868
  71.5 2.8 %copy-start.33 = (f32[256,8]{0,1:T(8,128)S(1)}, f32[256,8]{0,1:T(8,128)}, u32[]{:S(2)}) copy-start(f32[256,8]{0,1:T(8,128)} %get-tuple-element.110) | copy-start | bytes 24580
  71.5 2.8 %copy-start.14 = (f32[8,64,128]{2,1,0:T(8,128)S(1)}, f32[8,64,128]{2,1,0:T(8,128)}, u32[]{:S(2)}) copy-start(f32[8,64,128]{2,1,0:T(8,128)} %scan_ahead.1) | copy-start | bytes 786436
  112.1 6.5 %copy-start.13 = (bf16[1,256,512]{1,2,0:T(8,128)(2,1)S(1)}, bf16[1,256,512]{1,2,0:T(8,128)(2,1)}, u32[]{:S(2)}) copy-start(bf16[1,256,512]{1,2,0:T(8,128)(2,1)} %copy-done.12) | copy-start | bytes 786436
  112.2 6.5 %copy-start.31 = (f32[256,256]{1,0:T(8,128)S(1)}, f32[256,256]{1,0:T(8,128)}, u32[]{:S(2)}) copy-start(f32[256,256]{1,0:T(8,128)} %fusion.74) | copy-start | bytes 786436
  112.2 6.5 %copy-start.38 = (pred[256,256]{1,0:T(8,128)(4,1)S(1)}, pred[256,256]{1,0:T(8,128)(4,1)}, u32[]{:S(2)}) copy-start(pred[256,256]{1,0:T(8,128)(4,1)} %iota_compare_fusion) | copy-start | bytes 196612
  112.2 6.5 %copy-start.62 = (f32[256,8]{0,1:T(8,128)S(1)}, f32[256,8]{0,1:T(8,128)}, u32[]{:S(2)}) copy-start(f32[256,8]{0,1:T(8,128)} %get-tuple-element.138) | copy-start | bytes 24580
  112.2 6.5 %copy-start.66 = (f32[256,8]{0,1:T(8,128)S(1)}, f32[256,8]{0,1:T(8,128)}, u32[]{:S(2)}) copy-start(f32[256,8]{0,1:T(8,128)} %fusion.81) | copy-start | bytes 24580
  118.7 3.3 %copy-start.29 = (f32[256,128]{1,0:T(8,128)S(1)}, f32[256,128]{1,0:T(8,128)}, u32[]{:S(2)}) copy-start(f32[256,128]{1,0:T(8,128)} %convolution_bitcast_fusion) | copy-start | bytes 393220
  142.6 2.6 copy-start.42
  142.6 2.6 copy-start.64
  142.6 2.5 copy-start.65
  142.8 3.9 %copy-start.37 = (f32[256,8]{0,1:T(8,128)S(1)}, f32[256,8]{0,1:T(8,128)}, u32[]{:S(2)}) copy-start(f32[256,8]{0,1:T(8,128)} %copy-done.36) | copy-start | bytes 24580
  142.8 3.8 %copy-start.68 = (f32[256,8]{0,1:T(8,128)S(1)}, f32[256,8]{0,1:T(8,128)}, u32[]{:S(2)}) copy-start(f32[256,8]{0,1:T(8,128)} %get-tuple-element.86) | copy-start | bytes 24580
  142.8 3.8 %copy-start.71 = (f32[8]{0:T(128)S(1)}, f32[8]{0:T(128)}, u32[]{:S(2)}) copy-start(f32[8]{0:T(128)} %copy-done.70) | copy-start | bytes 100
  142.8 3.8 %copy-start.81 = (f32[8]{0:T(128)S(1)}, f32[8]{0:T(128)}, u32[]{:S(2)}) copy-start(f32[8]{0:T(128)} %copy-done.80) | copy-start | bytes 100
  142.9 4.7 %copy-start.20 = (bf16[256,512]{0,1:T(8,128)(2,1)S(1)}, bf16[256,512]{0,1:T(8,128)(2,1)}, u32[]{:S(2)}) copy-start(bf16[256,512]{0,1:T(8,128)(2,1)} %get-tuple-element.117) | copy-start | bytes 786436
  142.9 5.4 %copy-start.73 = (f32[1,3,256]{2,1,0:T(4,128)S(1)}, f32[1,3,256]{2,1,0:T(4,128)}, u32[]{:S(2)}) copy-start(f32[1,3,256]{2,1,0:T(4,128)} %pad_add_fusion.3) | copy-start | bytes 9220
  142.9 6.7 %copy-start.69 = (f32[512]{0:T(512)S(1)}, f32[512]{0:T(512)}, u32[]{:S(2)}) copy-start(f32[512]{0:T(512)} %get-tuple-element.116) | copy-start | bytes 6148
  142.9 6.7 %copy-start.74 = (f32[256]{0:T(256)S(1)}, f32[256]{0:T(256)}, u32[]{:S(2)}) copy-start(f32[256]{0:T(256)} %get-tuple-element.99) | copy-start | bytes 3076
  142.9 7.5 %copy-start.28 = (f32[1,259,256]{2,1,0:T(8,128)S(1)}, f32[1,259,256]{2,1,0:T(8,128)}, u32[]{:S(2)}) copy-start(f32[1,259,256]{2,1,0:T(8,128)} %pad_add_fusion.1) | copy-start | bytes 795652
  148.3 5.5 %collective-permute-start.3 = (f32[1,3,256]{2,1,0:T(4,128)S(1)}, f32[1,3,256]{2,1,0:T(4,128)S(1)}, u32[]{:S(2)}, u32[]{:S(2)}) collective-permute-start(f32[1,3,256]{2,1,0:T(4,128)S(1)} %copy-done.73), channel_id=1, source_target_pairs={{4,0},{8,4},{12,8},{16,12},{20,16},{24,20},{28,24},{5,1},{9,5},{13... | collective-permute-start | bytes 9224 | tf_op jit(solution)/shard_map/ppermute | solution.py:22
  150.4 11.5 %collective-permute-start.2 = (f32[1,3,512]{1,2,0:T(8,128)S(1)}, f32[1,3,512]{1,2,0:T(8,128)S(1)}, u32[]{:S(2)}, u32[]{:S(2)}) collective-permute-start(f32[1,3,512]{1,2,0:T(8,128)S(1)} %pad_add_fusion.2), channel_id=1, source_target_pairs={{4,0},{8,4},{12,8},{16,12},{20,16},{24,20},{28,24},{5,1},{9,5},{13... | collective-permute-start | bytes 18440 | tf_op jit(solution)/shard_map/ppermute | solution.py:22
  166.1 2.6 copy-start.15
  166.1 2.6 copy-start.56
  169.9 66.5 %copy-start.41 = (f32[1024]{0:T(1024)S(1)}, f32[1024]{0:T(1024)}, u32[]{:S(2)}) copy-start(f32[1024]{0:T(1024)} %param.19) | copy-start | bytes 12292
  169.9 66.5 %copy-start.54 = (f32[256]{0:T(256)S(1)}, f32[256]{0:T(256)}, u32[]{:S(2)}) copy-start(f32[256]{0:T(256)} %copy-done.53) | copy-start | bytes 3076
  234.6 35.4 %copy-start.72 = (f32[256]{0:T(256)S(1)}, f32[256]{0:T(256)}, u32[]{:S(2)}) copy-start(f32[256]{0:T(256)} %get-tuple-element.149) | copy-start | bytes 3076
  234.7 32.8 %copy-start.9 = (f32[4,128,128]{2,1,0:T(8,128)S(1)}, f32[4,128,128]{2,1,0:T(8,128)}, u32[]{:S(2)}) copy-start(f32[4,128,128]{2,1,0:T(8,128)} %copy-done.8) | copy-start | bytes 786436
  267.5 4.9 %copy-start.5 = (bf16[256,1024]{1,0:T(8,128)(2,1)S(1)}, bf16[256,1024]{1,0:T(8,128)(2,1)}, u32[]{:S(2)}) copy-start(bf16[256,1024]{1,0:T(8,128)(2,1)} %copy-done.4) | copy-start | bytes 1572868
  270.0 3.2 %copy-start.7 = (f32[512,128]{1,0:T(8,128)S(1)}, f32[512,128]{1,0:T(8,128)}, u32[]{:S(2)}) copy-start(f32[512,128]{1,0:T(8,128)} %copy-done.6) | copy-start | bytes 786436
  (28 other events, 42.2 us)
